TPU v7x, 128 devices: a whole 4x4x4 slice. The times are simulated.
128 devices in a mesh: replica: 8 (over x, y_hi), shard: 16 (over z, y_lo, core).
Axes of the slice: x: 4, y: 4 (y_hi: 2, y_lo: 2; y = y_hi * 2 + y_lo), z: 4, core: 2. Of those that a mesh axis runs over, the one named last changes fastest.
Arguments:
- tokens: bfloat16 [65536, 1920], P(('replica', 'shard')), may hold values from -36 to 36
- timesteps: int32 [256], P(('replica', 'shard')), may hold values from 0 to 63
- table: float32 [64, 2, 1920], replicated, may hold values from -3 to 3
- weight_values: bfloat16 [4864, 1920], P('shard'), may hold values from -0.125 to 0.125
- weight_scales: bfloat16 [4864, 15], P('shard'), may hold values from 0.29882812 to 3
- cotangent: bfloat16 [65536, 4864], P(('replica', 'shard')), may hold values from -24 to 24
Outputs:
- hidden: bfloat16 [65536, 4864], P(('replica', 'shard'))
- grad_weight: float32 [4864, 1920], P('shard')
- grad_tokens: bfloat16 [65536, 1920], P(('replica', 'shard'))
All inputs are finite; a program needn't handle non-finite values.
Results may differ from a plain program's by a relative error of at most 0.02.
Values may be sent and summed in bfloat16 or wider, within the bound.
A program may use at most 256 MiB of HBM per device.

v0:
```python
import jax
import jax.numpy as jnp
from jax import lax
from jax.sharding import PartitionSpec as P

root_two_over_pi = 0.7978845608028654
cubic_coef = 0.044715
epsilon = 1e-06


def gelu_slope(preact):
    inner_term = root_two_over_pi * (preact + cubic_coef * preact * preact * preact)
    tangent = jnp.tanh(inner_term)
    gelu_value = 0.5 * preact * (1.0 + tangent)
    derivative = 0.5 * (1.0 + tangent) + 0.5 * preact * (
        1.0 - tangent * tangent
    ) * root_two_over_pi * (1.0 + 3.0 * cubic_coef * preact * preact)
    return (gelu_value, derivative)


def dequantize(weight_values, weight_scales):
    row_count, features = weight_values.shape
    blocks = weight_scales.shape[1]
    expanded = (
        weight_values.astype(jnp.float32).reshape(row_count, blocks, features // blocks)
        * weight_scales.astype(jnp.float32)[:, :, None]
    )
    return expanded.reshape(row_count, features).astype(jnp.bfloat16)


def modulate(tokens, timesteps, table):
    samples = timesteps.shape[0]
    step_count = table.shape[0]
    features = tokens.shape[1]
    onehot = (timesteps[:, None] == jnp.arange(step_count, dtype=jnp.int32)[None, :]).astype(
        jnp.float32
    )
    picked = jnp.dot(
        onehot, table.reshape(step_count, 2 * features), precision=lax.Precision.HIGHEST
    )
    picked = picked.reshape(samples, 2, features)
    grouped = tokens.astype(jnp.float32).reshape(samples, -1, features)
    centre = grouped - jnp.mean(grouped, axis=2, keepdims=True)
    inverse = lax.rsqrt(jnp.mean(centre * centre, axis=2, keepdims=True) + epsilon)
    normed = centre * inverse
    factor = 1.0 + picked[:, 1][:, None, :]
    moved = (normed * factor + picked[:, 0][:, None, :]).reshape(-1, features).astype(jnp.bfloat16)
    return (moved, normed, inverse, factor)


def normalize_back(grad_moved, normed, inverse, factor):
    samples = normed.shape[0]
    features = normed.shape[2]
    scaled_grad = grad_moved.reshape(samples, -1, features) * factor
    mean_grad = jnp.mean(scaled_grad, axis=2, keepdims=True)
    mean_prod = jnp.mean(scaled_grad * normed, axis=2, keepdims=True)
    result = inverse * (scaled_grad - mean_grad - normed * mean_prod)
    return result.reshape(-1, features).astype(jnp.bfloat16)


def per_device(tokens, timesteps, table, weight_values, weight_scales, cotangent):
    moved, normed, inverse, factor = modulate(tokens, timesteps, table)
    upstream = cotangent.astype(jnp.float32)
    gathered_values, gathered_scales = (
        lax.all_gather(weight_values, "shard", axis=0, tiled=True),
        lax.all_gather(weight_scales, "shard", axis=0, tiled=True),
    )
    weight = dequantize(gathered_values, gathered_scales)
    preact = jnp.einsum("td,fd->tf", moved, weight, preferred_element_type=jnp.float32)
    gelu_value, derivative = gelu_slope(preact)
    hidden = gelu_value.astype(jnp.bfloat16)
    grad_pre = (upstream * derivative).astype(jnp.bfloat16)
    grad_moved = jnp.dot(grad_pre, weight, preferred_element_type=jnp.float32)
    product = lax.dot_general(
        grad_pre, moved, (((0,), (0,)), ((), ())), preferred_element_type=jnp.float32
    )
    rounded = lax.optimization_barrier(product.astype(jnp.bfloat16))
    group_part = lax.psum_scatter(
        rounded.astype(jnp.float32).astype(jnp.bfloat16), "shard", scatter_dimension=0, tiled=True
    )
    grad_weight = lax.psum(group_part, "replica").astype(jnp.float32)
    grad_tokens = normalize_back(grad_moved, normed, inverse, factor)
    return (hidden, grad_weight, grad_tokens)


def solution(mesh):
    placed = (
        P(("replica", "shard"), None),
        P(("replica", "shard")),
        P(),
        P("shard", None),
        P("shard", None),
        P(("replica", "shard"), None),
    )
    return jax.shard_map(
        per_device,
        mesh=mesh,
        in_specs=placed,
        out_specs=(P(("replica", "shard"), None), P("shard", None), P(("replica", "shard"), None)),
        check_vma=False,
    )
```

profile of v0, /device:TPU:0, one launch (start us, length us, event | category | flops | bytes accessed | tf_op | source)
XLA Modules:
  0.0 496.3 jit_solution(2334483835488481920)
XLA Ops:
  7.2 0.0 copy-start
  7.2 0.0 copy-start.3
  7.2 0.0 all-gather.3.cloned.1.call-start
  7.2 0.7 all-gather.3.cloned.1.call-update
  7.9 0.0 reduce-scatter.2.cloned.1.call-start
  8.0 22.6 %all-gather = bf16[16,304,15]{1,2,0:T(8,128)(2,1)S(1)} all-gather(bf16[1,304,15]{1,2,0:T(8,128)(2,1)} %bitcast.51), channel_id=1, replica_groups=mesh['replica'=8,'shard'=16] {'shard'}, dimensions={0}, use_global_device_ids=true | all-gather | bytes 155040 | tf_op jit(solution)/shard_map/all_gather | solution.py:66
  30.7 0.2 reshape.71
  30.9 0.0 copy-done
  30.9 0.0 copy-start.2
  30.9 0.3 convert_reduce_fusion
  31.3 0.7 multiply_reduce_fusion.1
  31.9 0.0 copy-done.3
  31.9 0.2 copy-done.2
  32.1 0.4 fusion.11
  32.6 2.5 fusion.10
  35.1 77.8 %all-gather.3.cloned.1.call-done = bf16[4864,1920]{1,0:T(8,128)(2,1)} async-done(((bf16[304,1920]{1,0:T(8,128)(2,1)}), bf16[4864,1920]{1,0:T(8,128)(2,1)}) %all-gather.3.cloned.1.call-update) | async-done | bytes 18677776 | tf_op jit(solution)/shard_map/all_gather | solution.py:65
  112.8 23.3 %copy.18 = bf16[4864,1920]{0,1:T(8,128)(2,1)} copy(bf16[4864,1920]{1,0:T(8,128)(2,1)} %all-gather.3.cloned.1.call-done) | data formatting | bytes 37355520 | tf_op jit(solution)/shard_map/all_gather | solution.py:65
  136.2 0.0 copy-start.1
  136.2 17.3 %fusion = bf16[4864,1920]{0,1:T(8,128)(2,1)} fusion(bf16[4864,1920]{0,1:T(8,128)(2,1)} %copy.18, f32[4864,15]{0,1:T(8,128)S(1)} %reshape.71), kind=kLoop, calls=%fused_computation.1 | loop fusion | flops 28016640 | bytes 37647360 | tf_op jit(solution)/shard_map/convert_element_type | solution.py:28
  153.5 0.0 copy-done.1
  153.5 21.5 %fusion.9 = (bf16[512,4864]{1,0:T(8,128)(2,1)S(1)}, bf16[512,4864]{1,0:T(8,128)(2,1)}) fusion(bf16[512,4864]{1,0:T(8,128)(2,1)} %param.11, bf16[512,1920]{1,0:T(8,128)(2,1)S(1)} %copy-done.1, bf16[4864,1920]{0,1:T(8,128)(2,1)} %fusion), kind=kOutput, calls=%fused_computation.13 | convolution fusion | flops 9617801216 | bytes 35586048 | tf_op jit(solution)/shard_map/td,fd->tf/dot_general | solution.py:69
  175.0 0.0 copy-start.4
  175.0 2.2 copy-done.4
  177.3 15.2 %convolution_convert_fusion = bf16[4864,1920]{1,0:T(8,128)(2,1)} fusion(bf16[512,4864]{1,0:T(8,128)(2,1)S(1)} %get-tuple-element.5, bf16[512,1920]{1,0:T(8,128)(2,1)S(1)} %copy-done.1), kind=kOutput, calls=%fused_computation.2 | convolution fusion | flops 9572352000 | bytes 25624576 | tf_op jit(solution)/shard_map/dot_general | solution.py:74
  192.5 0.0 reduce-scatter.2.cloned.1.call-update
  192.5 0.0 all-reduce.2.cloned.1.call-start
  192.6 203.4 %reduce-scatter.2.cloned.1.call-done = bf16[304,1920]{1,0:T(8,128)(2,1)} async-done(((bf16[4864,1920]{1,0:T(8,128)(2,1)}), bf16[304,1920]{1,0:T(8,128)(2,1)}) %reduce-scatter.2.cloned.1.call-update) | async-done | bytes 1167376 | tf_op jit(solution)/shard_map/reduce_scatter | solution.py:78
  396.0 0.0 all-reduce.2.cloned.1.call-update
  396.0 17.9 %multiply_reduce_fusion.2 = (f32[2,256]{1,0:T(2,128)S(1)}, f32[2,256]{1,0:T(2,128)S(1)}, f32[2,256,1920]{2,1,0:T(8,128)}) fusion(f32[2,1920]{1,0:T(2,128)S(1)} %get-tuple-element.7, f32[2,256]{1,0:T(2,128)S(1)} %rsqrt.13, f32[2,256]{1,0:T(2,128)S(1)} %div.17, bf16[2,256,4864]{2,1,0:T(8,128)(2,1)} %bitcast.52, bf16[4864,1920]{0,1:T(8,128)(2,1)} %fusion, ...), kind=kOutput, calls=%fused_computation.22 | convolution fusion | flops 9569894400 | bytes 29580288 | tf_op jit(solution)/shard_map/dot_general | solution.py:73
  413.9 3.9 multiply_convert_fusion.1
  417.7 69.2 %all-reduce.2.cloned.1.call-done = bf16[304,1920]{1,0:T(8,128)(2,1)} async-done(((bf16[304,1920]{1,0:T(8,128)(2,1)}), bf16[304,1920]{1,0:T(8,128)(2,1)}) %all-reduce.2.cloned.1.call-update) | async-done | bytes 1167376 | tf_op jit(solution)/shard_map/psum | solution.py:81
  487.0 2.8 convert_element_type.48
  (7 shorter events, 0.1 us)
Async XLA Ops:
  7.2 23.7 %copy-start = (bf16[512,1920]{1,0:T(8,128)(2,1)S(1)}, bf16[512,1920]{1,0:T(8,128)(2,1)}, u32[]{:S(2)}) copy-start(bf16[512,1920]{1,0:T(8,128)(2,1)} %param.6) | copy-start | bytes 5898244
  7.2 24.8 %copy-start.3 = (s32[2]{0:T(128)S(1)}, s32[2]{0:T(128)}, u32[]{:S(2)}) copy-start(s32[2]{0:T(128)} %param.7) | copy-start | bytes 28
  7.2 105.7 %all-gather.3.cloned.1.call-start = ((), (), s32[]{:S(2)}) async-start(), calls=%async_computation.1 | async-start | bytes 19845120 | tf_op jit(solution)/shard_map/all_gather | solution.py:65
  7.9 388.0 %reduce-scatter.2.cloned.1.call-start = ((), (), s32[]{:S(2)}) async-start(), calls=%async_computation.2 | async-start | bytes 19845120 | tf_op jit(solution)/shard_map/reduce_scatter | solution.py:78
  30.9 1.2 copy-start.2
  136.2 17.3 %copy-start.1 = (bf16[512,1920]{1,0:T(8,128)(2,1)S(1)}, bf16[512,1920]{1,0:T(8,128)(2,1)}, u32[]{:S(2)}) copy-start(bf16[512,1920]{1,0:T(8,128)(2,1)} %fusion.10) | copy-start | bytes 5898244
  175.0 2.2 copy-start.4
  192.5 294.4 %all-reduce.2.cloned.1.call-start = ((), (), s32[]{:S(2)}) async-start(), calls=%async_computation.3 | async-start | bytes 2334720 | tf_op jit(solution)/shard_map/psum | solution.py:81
Sparse Core Ops, SparseCore 0:
  9.7 103.0 all-gather.2
  192.6 203.2 reduce-scatter.1
  398.6 88.2 all-reduce.1
where the time goes:
time: 497 us; the launch traced here: 496 us
  waiting for transfers between devices  351 us (71%)
  matrix products  55.1 us (11%)
  other arithmetic  27.5 us (6%)
  local copies, waits for them, and re-layouts  26 us (5%)
  blocking collectives  22.6 us (5%)
  between operations  13.8 us (3%)
    reduce_scatter x1, waiting for transfers between devices, per_device(): lax.psum_scatter(rounded.astype(jnp.float32).astype(jnp.bfloat16), 'shard...  203 us
    all_gather x1, waiting for transfers between devices, per_device(): lax.all_gather(weight_values, 'shard', axis=0, tiled=True)  77.8 us
    psum x1, waiting for transfers between devices, per_device(): grad_weight = lax.psum(group_part, 'replica').astype(jnp.float32)  69.2 us
    all_gather x1, local copies, waits for them, and re-layouts, per_device(): lax.all_gather(weight_values, 'shard', axis=0, tiled=True)  23.3 us
    all_gather x1, blocking collectives, per_device(): lax.all_gather(weight_scales, 'shard', axis=0, tiled=True)  22.6 us
    dot_general x1, matrix products, per_device(): jnp.einsum('td,fd->tf', moved, weight, preferred_element_type=jnp.float32)  21.5 us
    dot_general x1, matrix products, per_device(): grad_moved = jnp.dot(grad_pre, weight, preferred_element_type=jnp.float32)  17.9 us
    convert_element_type x1, other arithmetic, dequantize(): return expanded.reshape(row_count, features).astype(jnp.bfloat16)  17.3 us
  transfers between devices with their start and end apart: 3, of which 3 were waited for; matrix products, arithmetic and copies ran while one was open for 5% of the time, Pallas kernels for 0%

commit v1 on v0

--- a/solution.py
+++ b/solution.py
@@ -2,10 +2,16 @@
 import jax.numpy as jnp
 from jax import lax
 from jax.sharding import PartitionSpec as P
+from jax.lax import all_gather
 
 root_two_over_pi = 0.7978845608028654
 cubic_coef = 0.044715
 epsilon = 1e-06
+
+
+def map_streams(my_tile):
+    state_next = jnp.sum(all_gather(my_tile, "replica"), axis=0)
+    return state_next
 
 
 def gelu_slope(preact):
@@ -78,7 +84,7 @@
     group_part = lax.psum_scatter(
         rounded.astype(jnp.float32).astype(jnp.bfloat16), "shard", scatter_dimension=0, tiled=True
     )
-    grad_weight = lax.psum(group_part, "replica").astype(jnp.float32)
+    grad_weight = map_streams(group_part).astype(jnp.float32)
     grad_tokens = normalize_back(grad_moved, normed, inverse, factor)
     return (hidden, grad_weight, grad_tokens)
 

time: 497 us -> 530 us (1.066)
  waiting for transfers between devices: 351 us -> 379 us
    all_gather x0 -> x1, waiting for transfers between devices: none -> 97 us  [map_streams(): state_next = jnp.sum(all_gather(my_tile, 'replica'), axis=0)]
    psum x1 -> x0, waiting for transfers between devices: 69.2 us -> none  [per_device(): grad_weight = lax.psum(group_part, 'replica').astype(jnp.float32)]
    reduce_sum x0 -> x1, other arithmetic: none -> 5.53 us  [map_streams(): state_next = jnp.sum(all_gather(my_tile, 'replica'), axis=0)]
where the time goes in v1:
time: 530 us; the launch traced here: 528 us
  waiting for transfers between devices  379 us (72%)
  matrix products  55.1 us (10%)
  other arithmetic  31.8 us (6%)
  local copies, waits for them, and re-layouts  26 us (5%)
  blocking collectives  22.6 us (4%)
  between operations  13.8 us (3%)
    reduce_scatter x1, waiting for transfers between devices, per_device(): lax.psum_scatter(rounded.astype(jnp.float32).astype(jnp.bfloat16), 'shard...  203 us
    all_gather x1, waiting for transfers between devices, map_streams(): state_next = jnp.sum(all_gather(my_tile, 'replica'), axis=0)  97 us
    all_gather x1, waiting for transfers between devices, per_device(): lax.all_gather(weight_values, 'shard', axis=0, tiled=True)  77.8 us
    all_gather x1, local copies, waits for them, and re-layouts, per_device(): lax.all_gather(weight_values, 'shard', axis=0, tiled=True)  23.3 us
    all_gather x1, blocking collectives, per_device(): lax.all_gather(weight_scales, 'shard', axis=0, tiled=True)  22.6 us
    dot_general x1, matrix products, per_device(): jnp.einsum('td,fd->tf', moved, weight, preferred_element_type=jnp.float32)  21.5 us
    dot_general x1, matrix products, per_device(): grad_moved = jnp.dot(grad_pre, weight, preferred_element_type=jnp.float32)  17.9 us
    convert_element_type x1, other arithmetic, dequantize(): return expanded.reshape(row_count, features).astype(jnp.bfloat16)  17.3 us
  transfers between devices with their start and end apart: 3, of which 3 were waited for; matrix products, arithmetic and copies ran while one was open for 5% of the time, Pallas kernels for 0%

profile of v1, /device:TPU:0, one launch (start us, length us, event | category | flops | bytes accessed | tf_op | source)
XLA Modules:
  0.0 528.4 jit_solution(6311239397062002841)
XLA Ops:
  7.2 0.0 copy-start
  7.2 0.0 copy-start.3
  7.2 0.0 all-gather.5.cloned.1.call-start
  7.2 0.7 all-gather.5.cloned.1.call-update
  7.9 0.0 reduce-scatter.2.cloned.1.call-start
  8.0 22.6 %all-gather.1 = bf16[16,304,15]{1,2,0:T(8,128)(2,1)S(1)} all-gather(bf16[1,304,15]{1,2,0:T(8,128)(2,1)} %bitcast.53), channel_id=1, replica_groups=mesh['replica'=8,'shard'=16] {'shard'}, dimensions={0}, use_global_device_ids=true | all-gather | bytes 155040 | tf_op jit(solution)/shard_map/all_gather | solution.py:72
  30.7 0.2 reshape.72
  30.9 0.0 copy-done
  30.9 0.0 copy-start.2
  30.9 0.3 convert_reduce_fusion
  31.3 0.7 multiply_reduce_fusion.1
  31.9 0.0 copy-done.3
  31.9 0.2 copy-done.2
  32.1 0.4 fusion.11
  32.6 2.5 fusion.10
  35.1 77.8 %all-gather.5.cloned.1.call-done = bf16[4864,1920]{1,0:T(8,128)(2,1)} async-done(((bf16[304,1920]{1,0:T(8,128)(2,1)}), bf16[4864,1920]{1,0:T(8,128)(2,1)}) %all-gather.5.cloned.1.call-update) | async-done | bytes 18677776 | tf_op jit(solution)/shard_map/all_gather | solution.py:71
  112.8 23.3 %copy.18 = bf16[4864,1920]{0,1:T(8,128)(2,1)} copy(bf16[4864,1920]{1,0:T(8,128)(2,1)} %all-gather.5.cloned.1.call-done) | data formatting | bytes 37355520 | tf_op jit(solution)/shard_map/all_gather | solution.py:71
  136.2 0.0 copy-start.1
  136.2 17.3 %fusion = bf16[4864,1920]{0,1:T(8,128)(2,1)} fusion(bf16[4864,1920]{0,1:T(8,128)(2,1)} %copy.18, f32[4864,15]{0,1:T(8,128)S(1)} %reshape.72), kind=kLoop, calls=%fused_computation.1 | loop fusion | flops 28016640 | bytes 37647360 | tf_op jit(solution)/shard_map/convert_element_type | solution.py:34
  153.5 0.0 copy-done.1
  153.5 21.5 %fusion.9 = (bf16[512,4864]{1,0:T(8,128)(2,1)S(1)}, bf16[512,4864]{1,0:T(8,128)(2,1)}) fusion(bf16[512,4864]{1,0:T(8,128)(2,1)} %param.11, bf16[512,1920]{1,0:T(8,128)(2,1)S(1)} %copy-done.1, bf16[4864,1920]{0,1:T(8,128)(2,1)} %fusion), kind=kOutput, calls=%fused_computation.13 | convolution fusion | flops 9617801216 | bytes 35586048 | tf_op jit(solution)/shard_map/td,fd->tf/dot_general | solution.py:75
  175.0 0.0 copy-start.4
  175.0 2.2 copy-done.4
  177.3 15.2 %convolution_convert_fusion = bf16[4864,1920]{1,0:T(8,128)(2,1)} fusion(bf16[512,4864]{1,0:T(8,128)(2,1)S(1)} %get-tuple-element.5, bf16[512,1920]{1,0:T(8,128)(2,1)S(1)} %copy-done.1), kind=kOutput, calls=%fused_computation.2 | convolution fusion | flops 9572352000 | bytes 25624576 | tf_op jit(solution)/shard_map/dot_general | solution.py:80
  192.5 0.0 reduce-scatter.2.cloned.1.call-update
  192.5 0.0 all-gather.7.cloned.1.call-start
  192.6 203.4 %reduce-scatter.2.cloned.1.call-done = bf16[304,1920]{1,0:T(8,128)(2,1)} async-done(((bf16[4864,1920]{1,0:T(8,128)(2,1)}), bf16[304,1920]{1,0:T(8,128)(2,1)}) %reduce-scatter.2.cloned.1.call-update) | async-done | bytes 1167376 | tf_op jit(solution)/shard_map/reduce_scatter | solution.py:84
  396.0 0.0 all-gather.7.cloned.1.call-update
  396.0 17.9 %multiply_reduce_fusion.2 = (f32[2,256]{1,0:T(2,128)S(1)}, f32[2,256]{1,0:T(2,128)S(1)}, f32[2,256,1920]{2,1,0:T(8,128)}) fusion(f32[2,1920]{1,0:T(2,128)S(1)} %get-tuple-element.7, f32[2,256]{1,0:T(2,128)S(1)} %rsqrt.13, f32[2,256]{1,0:T(2,128)S(1)} %div.17, bf16[2,256,4864]{2,1,0:T(8,128)(2,1)} %bitcast.54, bf16[4864,1920]{0,1:T(8,128)(2,1)} %fusion, ...), kind=kOutput, calls=%fused_computation.22 | convolution fusion | flops 9569894400 | bytes 29580288 | tf_op jit(solution)/shard_map/dot_general | solution.py:79
  413.9 3.9 multiply_convert_fusion.1
  417.8 97.0 %all-gather.7.cloned.1.call-done = bf16[2432,1920]{1,0:T(8,128)(2,1)} async-done(((bf16[304,1920]{1,0:T(8,128)(2,1)}), bf16[2432,1920]{1,0:T(8,128)(2,1)}) %all-gather.7.cloned.1.call-update) | async-done | bytes 9338896 | tf_op jit(solution)/shard_map/all_gather | solution.py:13
  514.8 5.5 %reduce_sum.50 = bf16[304,1920]{1,0:T(8,128)(2,1)S(1)} reduce(bf16[8,304,1920]{2,1,0:T(8,128)(2,1)} %bitcast.50, bf16[]{:T(256)} %constant.22.clone.1), dimensions={0}, to_apply=%region_3.0 | reduce | flops 4085760 | bytes 10506242 | tf_op jit(solution)/shard_map/reduce_sum | solution.py:13
  520.3 1.5 convert_element_type.50
  (7 shorter events, 0.1 us)
Async XLA Ops:
  7.2 23.7 %copy-start = (bf16[512,1920]{1,0:T(8,128)(2,1)S(1)}, bf16[512,1920]{1,0:T(8,128)(2,1)}, u32[]{:S(2)}) copy-start(bf16[512,1920]{1,0:T(8,128)(2,1)} %param.6) | copy-start | bytes 5898244
  7.2 24.8 %copy-start.3 = (s32[2]{0:T(128)S(1)}, s32[2]{0:T(128)}, u32[]{:S(2)}) copy-start(s32[2]{0:T(128)} %param.7) | copy-start | bytes 28
  7.2 105.7 %all-gather.5.cloned.1.call-start = ((), (), s32[]{:S(2)}) async-start(), calls=%async_computation.1 | async-start | bytes 19845120 | tf_op jit(solution)/shard_map/all_gather | solution.py:71
  7.9 388.0 %reduce-scatter.2.cloned.1.call-start = ((), (), s32[]{:S(2)}) async-start(), calls=%async_computation.2 | async-start | bytes 19845120 | tf_op jit(solution)/shard_map/reduce_scatter | solution.py:84
  30.9 1.2 copy-start.2
  136.2 17.3 %copy-start.1 = (bf16[512,1920]{1,0:T(8,128)(2,1)S(1)}, bf16[512,1920]{1,0:T(8,128)(2,1)}, u32[]{:S(2)}) copy-start(bf16[512,1920]{1,0:T(8,128)(2,1)} %fusion.10) | copy-start | bytes 5898244
  175.0 2.2 copy-start.4
  192.5 322.3 %all-gather.7.cloned.1.call-start = ((), (), s32[]{:S(2)}) async-start(), calls=%async_computation.3 | async-start | bytes 10506240 | tf_op jit(solution)/shard_map/all_gather | solution.py:13
Sparse Core Ops, SparseCore 0:
  9.7 103.0 all-gather.4
  192.6 203.2 reduce-scatter.1
  398.6 116.1 all-gather.6
